TPU v7x, 32 devices: a whole 2x2x4 slice. The times are simulated.
32 devices in a mesh: segment: 2 (over core), clip: 4 (over z), tile: 4 (over y, x).
Axes of the slice: x: 2, y: 2, z: 4, core: 2. Of those that a mesh axis runs over, the one named last changes fastest.
Arguments:
- video: bfloat16 [4, 4, 3, 12, 4, 256], P('clip', 'tile'), may hold values from -6 to 6
- cotangent: bfloat16 [4, 4, 3, 12, 4, 256], P('clip', 'tile'), may hold values from -6 to 6
- weights: bfloat16 [2, 27, 256, 256], P('segment'), may hold values from -0.078125 to 0.078125
- neighbours: int32 [4, 4, 2], P('clip', 'tile'), may hold values from 0 to 4, as said below
- rows_used: int32 [4, 4], P('clip', 'tile'), may hold values from 3 to 12, as said below
- cols_used: int32 [4], P('clip'), may hold values from 2 to 4, as said below
Outputs:
- section_out: bfloat16 [2, 4, 4, 3, 12, 4, 256], P('segment', 'clip', 'tile')
- grads: float32 [2, 3, 589824], P('segment', None, ('clip', 'tile'))
Inputs may be any that keep to these rules, and one draw needn't show every extreme that they name: `neighbours`: in each clip the strips of its frames lie on the 4 tiles in an order of their own: entry 0 names the tile of the strip above, entry 1 the tile of the strip below, 4 where there is none; exactly one strip of each clip has none above and one has none below, and the entries chain all 4 strips of a clip top to bottom. `rows_used`: in every clip some strip has 12 rows. `cols_used`: some clip has 4 columns.
All inputs are finite; a program needn't handle non-finite values.
Results may differ from a plain program's by a relative error of at most 0.0054.
Values may be sent and summed in bfloat16 or wider, within the bound.
A program may use at most 576 MiB of HBM per device.

v0:
```python
import jax
import jax.numpy as jnp
from jax import lax
from jax.sharding import PartitionSpec as P


def shifted(block, axis, distance):
    devices = range(lax.axis_size(axis))
    route = [(i - distance, i) for i in devices if i - distance in devices]
    return lax.ppermute(block, axis, route)


def silu_grad(values):
    sigmoid = jax.nn.sigmoid(values)
    return sigmoid * (1.0 + values * (1.0 - sigmoid))


def pad_block(strip_field, upper, bottom, row_count):
    frame_count, height, columns, channels = strip_field.shape
    blank = jnp.zeros((frame_count, 1, columns, channels), strip_field.dtype)
    padded = jnp.concatenate([upper[:, None], strip_field, blank], axis=1)
    padded = lax.dynamic_update_slice_in_dim(padded, bottom[:, None], row_count + 1, axis=1)
    return jnp.pad(padded, ((0, 0), (0, 0), (1, 1), (0, 0)))


def patches(stacked, frame_count, height, columns):
    pieces = []
    for depth_off in range(3):
        for row_off in range(3):
            for col_off in range(3):
                pieces.append(
                    stacked[
                        depth_off : depth_off + frame_count,
                        row_off : row_off + height,
                        col_off : col_off + columns,
                    ]
                )
    return jnp.concatenate(pieces, axis=-1).reshape(frame_count * height * columns, -1)


def every_tap_entries(patch_fwd, weighting, start, count, channels):
    span = 9 * channels
    row_total = min(count // channels + 2, span)
    row_low = jnp.minimum(start // channels, span - row_total)
    columns = jnp.concatenate(
        [
            lax.dynamic_slice_in_dim(patch_fwd, tap * span + row_low, row_total, 1)
            for tap in range(3)
        ],
        axis=1,
    )
    contract = (((0,), (0,)), ((), ()))
    block = lax.dot_general(
        columns, weighting, contract, preferred_element_type=jnp.float32
    ).reshape(3, -1)
    return block.T


def local(video, cotangent, weights, neighbours, rows_used, cols_used):
    window = video[0, 0]
    frame_count, height, columns, channels = window.shape
    tile_count = lax.axis_size("tile")
    section = lax.axis_index("segment")
    row_count = rows_used[0, 0]
    col_count = cols_used[0]
    upper_tile = neighbours[0, 0, 0]
    lower_tile = neighbours[0, 0, 1]
    row_ids = jnp.arange(height, dtype=jnp.int32)
    col_ids = jnp.arange(columns, dtype=jnp.int32)
    inside = (row_ids[:, None] < row_count) & (col_ids[None, :] < col_count)
    inside_mask = inside[None, :, :, None]
    kernel = weights[0]
    forward_mat = kernel.reshape(27 * channels, channels)
    backward_mat = kernel[::-1].transpose(0, 2, 1).reshape(27 * channels, channels)
    front_zero = jnp.zeros((2, height + 2, columns + 2, channels), jnp.bfloat16)

    def halo_block(field):
        leading = field[:, 0]
        trailing = lax.dynamic_index_in_dim(field, row_count - 1, axis=1, keepdims=False)
        both_rows = jnp.stack([leading, trailing], axis=1)
        gathered = lax.all_gather(both_rows[None], "tile", axis=0, tiled=True)
        upper = gathered[jnp.minimum(upper_tile, tile_count - 1), :, 1]
        bottom = gathered[jnp.minimum(lower_tile, tile_count - 1), :, 0]
        upper = jnp.where(upper_tile < tile_count, upper, jnp.zeros_like(upper))
        bottom = jnp.where(lower_tile < tile_count, bottom, jnp.zeros_like(bottom))
        return pad_block(field, upper, bottom, row_count)

    def advance(entry, history):
        count = entry.shape[0]
        activated = jax.nn.silu(entry.astype(jnp.float32)).astype(jnp.bfloat16)
        padded = halo_block(activated)
        stacked = jnp.concatenate([history, padded], axis=0)
        mixed = jnp.dot(
            patches(stacked, count, height, columns),
            forward_mat,
            preferred_element_type=jnp.float32,
        ).reshape(entry.shape)
        result = jnp.where(inside_mask, entry.astype(jnp.float32) + mixed, 0.0).astype(jnp.bfloat16)
        return (result, stacked[-2:], padded)

    source = jnp.where(inside_mask, window, jnp.zeros_like(window))
    is_encoder = section == 0
    first_out, first_hist, first_pad = advance(source, front_zero)
    latent = shifted(first_out, "segment", 1)
    second_out, second_hist, second_pad = advance(latent, front_zero)
    own_out = jnp.where(is_encoder, first_out, second_out)
    own_input = jnp.where(is_encoder, source, latent)
    own_pad = jnp.where(is_encoder, first_pad, second_pad)
    target = jnp.where(inside_mask, cotangent[0, 0], jnp.zeros_like(cotangent[0, 0]))
    patch_fwd = patches(
        jnp.concatenate([front_zero, own_pad], axis=0), frame_count, height, columns
    )
    back_stack = jnp.concatenate([halo_block(target), front_zero], axis=0)
    spread = jnp.dot(
        patches(back_stack, frame_count, height, columns),
        backward_mat,
        preferred_element_type=jnp.float32,
    ).reshape(target.shape)
    own_grad = jnp.where(
        inside_mask,
        target.astype(jnp.float32) + silu_grad(own_input.astype(jnp.float32)) * spread,
        0.0,
    ).astype(jnp.bfloat16)
    returned = shifted(own_grad, "segment", -1)
    weighting = jnp.where(is_encoder, returned, target).reshape(-1, channels)
    flat_rows = 9 * channels * channels // lax.axis_size(("clip", "tile"))
    shares = lax.psum_scatter(
        every_tap_entries(
            patch_fwd,
            weighting,
            jnp.int32(0),
            flat_rows * lax.axis_size(("clip", "tile")),
            channels,
        ),
        ("clip", "tile"),
        scatter_dimension=0,
        tiled=True,
    )
    summed = shares.T
    return (own_out[None, None, None], summed[None])


def solution(mesh):
    in_specs = (
        P("clip", "tile", None, None, None, None),
        P("clip", "tile", None, None, None, None),
        P("segment", None, None, None),
        P("clip", "tile", None),
        P("clip", "tile"),
        P("clip"),
    )
    out_specs = (
        P("segment", "clip", "tile", None, None, None, None),
        P("segment", None, ("clip", "tile")),
    )
    return jax.shard_map(local, mesh=mesh, in_specs=in_specs, out_specs=out_specs, check_vma=False)
```

profile of v0, /device:TPU:0, one launch (start us, length us, event | category | flops | bytes accessed | tf_op | source)
XLA Modules:
  0.0 367.3 jit_solution(6660135488782941422)
XLA Ops:
  7.2 0.0 all-reduce.10.cloned.1.call-start
  7.2 1.3 fusion.28
  12.4 0.1 broadcast_and_fusion
  12.5 1.0 bitcast_select_fusion
  13.5 1.0 fusion.18
  14.6 9.7 %all-gather.2 = bf16[12,2,4,256]{3,2,1,0:T(4,128)(2,1)S(1)} all-gather(bf16[3,2,4,256]{3,2,1,0:T(4,128)(2,1)S(1)} %copy.127), channel_id=4, replica_groups=mesh['segment'=2,'clip'=4,'tile'=4] {'tile'}, dimensions={0}, use_global_device_ids=true | all-gather | bytes 61440 | tf_op jit(solution)/shard_map/all_gather | solution.py:81
  24.4 8.2 %all-gather = bf16[12,2,4,256]{3,2,1,0:T(4,128)(2,1)S(1)} all-gather(bf16[3,2,4,256]{3,2,1,0:T(4,128)(2,1)S(1)} %copy.120), channel_id=2, replica_groups=mesh['segment'=2,'clip'=4,'tile'=4] {'tile'}, dimensions={0}, use_global_device_ids=true | all-gather | bytes 61440 | tf_op jit(solution)/shard_map/all_gather | solution.py:81
  32.7 0.1 pad.29.clone
  32.8 0.1 maximum_maximum_fusion.2
  32.9 0.1 dynamic_update_slice.9
  33.7 1.4 copy-done
  35.0 0.9 fusion.2
  35.9 1.3 collective-permute-start
  37.2 0.1 dynamic_update_slice.11
  37.4 5.7 %copy.130 = bf16[1,27,256,256]{2,3,1,0:T(8,128)(2,1)} copy(bf16[1,27,256,256]{3,2,1,0:T(8,128)(2,1)} %param.8) | data formatting | bytes 7077888 | tf_op args[2]
  43.7 4.2 %rev.3 = bf16[27,256,256]{1,2,0:T(8,128)(2,1)} reverse(bf16[27,256,256]{1,2,0:T(8,128)(2,1)} %bitcast.80), dimensions={0} | reverse | bytes 7077888 | tf_op jit(solution)/shard_map/rev | solution.py:74
  48.0 3.0 fusion.14
  51.0 7.3 %all-gather.1 = bf16[12,2,4,256]{3,2,1,0:T(4,128)(2,1)S(1)} all-gather(bf16[3,2,4,256]{3,2,1,0:T(4,128)(2,1)S(1)} %copy.123), channel_id=3, replica_groups=mesh['segment'=2,'clip'=4,'tile'=4] {'tile'}, dimensions={0}, use_global_device_ids=true | all-gather | bytes 61440 | tf_op jit(solution)/shard_map/all_gather | solution.py:81
  58.3 0.1 maximum_maximum_fusion.1
  58.4 0.1 dynamic_update_slice.10
  59.2 1.5 collective-permute-start.1
  60.7 1.7 collective-permute-done.1
  62.4 4.0 %convolution_bitcast_fusion = f32[6912,256]{1,0:T(8,128)} fusion(bf16[3,12,4,6912]{3,1,2,0:T(8,128)(2,1)S(1)} %constant_dynamic-update-slice_fusion.54, bf16[3,12,4,256]{3,1,2,0:T(8,128)(2,1)S(1)} %collective-permute-done.1, pred[]{:T(512)S(6)} %eq.3, bf16[1,1,3,12,4,256]{5,4,3,2,1,0:T(4,128)(2,1)S(1)} %copy-done.3, pred[12,4]{0,1:T(4,128)(4,1)S(1)} %broadcast_and_fusion), kind=kOutput, calls=%fused_computation | convolution fusion | flops 509681664 | bytes 9216049 | tf_op jit(solution)/shard_map/dot_general | solution.py:53
  66.4 10.6 %reshape.152 = f32[3,589824]{1,0:T(4,128)} reshape(f32[6912,256]{1,0:T(8,128)} %convolution_bitcast_fusion) | data formatting | bytes 14155776 | tf_op jit(solution)/shard_map/reshape | solution.py:55
  77.0 0.6 copy-done.4
  77.6 0.6 dynamic-slice
  79.5 1.4 copy-done.1
  80.9 0.9 fusion.5
  81.8 0.7 copy.131
  82.5 275.6 %all-reduce.10.cloned.1.call-done = f32[589824,3]{0,1:T(4,128)} async-done(((f32[589824,3]{0,1:T(4,128)}), f32[589824,3]{0,1:T(4,128)}) %all-reduce.10.cloned.1.call-update) | async-done | bytes 7077904
  358.1 1.2 dynamic-slice_bitcast_fusion
  359.2 1.2 copy.132
  (139 shorter events, 2.2 us)
Async XLA Ops:
  7.2 350.9 %all-reduce.10.cloned.1.call-start = ((), (), s32[]{:S(2)}) async-start(), calls=%async_computation | async-start | bytes 18874368
  33.0 2.0 copy-start
  33.1 2.0 copy-start.2
  35.9 12.0 %collective-permute-start = (bf16[3,12,4,256]{3,1,2,0:T(8,128)(2,1)S(1)}, bf16[3,12,4,256]{3,1,2,0:T(8,128)(2,1)S(1)}, u32[]{:S(2)}, u32[]{:S(2)}) collective-permute-start(bf16[3,12,4,256]{3,1,2,0:T(8,128)(2,1)S(1)} %fusion.2), channel_id=1, source_target_pairs={{0,16},{1,17},{2,18},{3,19},{4,20},{5,21},{6,22},{7,23},{8,24},{9,... | collective-permute-start | bytes 221192 | tf_op jit(solution)/shard_map/ppermute | solution.py:10
  43.7 4.2 %copy-start.3 = (bf16[1,1,3,12,4,256]{5,4,3,2,1,0:T(4,128)(2,1)S(1)}, bf16[1,1,3,12,4,256]{5,4,3,2,1,0:T(4,128)(2,1)}, u32[]{:S(2)}) copy-start(bf16[1,1,3,12,4,256]{5,4,3,2,1,0:T(4,128)(2,1)} %param.7) | copy-start | bytes 221188
  59.2 3.2 collective-permute-start.1
  77.0 0.7 copy-start.4
  78.9 2.0 copy-start.1
Sparse Core Ops, SparseCore 0:
  77.1 280.8 all-reduce.9
where the time goes:
time: 368 us; the launch traced here: 367 us
  waiting for transfers between devices  277 us (75%)
  local copies, waits for them, and re-layouts  31.2 us (8%)
  blocking collectives  25.2 us (7%)
  between operations  19.7 us (5%)
  matrix products  8.71 us (2%)
    unnamed x2, waiting for transfers between devices  276 us
    all_gather x3, blocking collectives, halo_block(): gathered = lax.all_gather(both_rows[None], 'tile', axis=0, tiled=True)  25.2 us
    unnamed x118, local copies, waits for them, and re-layouts  13.4 us
    reshape x1, local copies, waits for them, and re-layouts, every_tap_entries(): block = lax.dot_general(columns, weighting, contract, preferred_element_t...  10.6 us
  transfers between devices with their start and end apart: 3, of which 2 were waited for; matrix products, arithmetic and copies ran while one was open for 4% of the time, Pallas kernels for 0%

commit v1 on v0

--- a/solution.py
+++ b/solution.py
@@ -78,7 +78,14 @@
         leading = field[:, 0]
         trailing = lax.dynamic_index_in_dim(field, row_count - 1, axis=1, keepdims=False)
         both_rows = jnp.stack([leading, trailing], axis=1)
-        gathered = lax.all_gather(both_rows[None], "tile", axis=0, tiled=True)
+        ring = [both_rows[None]]
+        for hop in range(3):
+            ring.append(lax.ppermute(ring[-1], "tile", [(dev, (dev + 1) % 4) for dev in range(4)]))
+        gathered = jnp.roll(
+            jnp.concatenate(ring[::-1], axis=0),
+            (lax.axis_index("tile") + 1) * ring[0].shape[0],
+            axis=0,
+        )
         upper = gathered[jnp.minimum(upper_tile, tile_count - 1), :, 1]
         bottom = gathered[jnp.minimum(lower_tile, tile_count - 1), :, 0]
         upper = jnp.where(upper_tile < tile_count, upper, jnp.zeros_like(upper))

time: 368 us -> 367 us (level)
  blocking collectives: 25.2 us -> 0 us
  waiting for transfers between devices: 277 us -> 292 us
  starting transfers between devices: 2.81 us -> 12.6 us
    all_gather x3 -> x0, blocking collectives: 25.2 us -> none  [halo_block(): gathered = lax.all_gather(both_rows[None], 'tile', axis=0, tiled=True)]
    ppermute x0 -> x9, waiting for transfers between devices: none -> 17.1 us  [halo_block(): lax.ppermute(ring[-1], 'tile', [(dev, (dev + 1) % 4) for dev in range(4)])]
    ppermute x0 -> x9, starting transfers between devices: none -> 9.99 us  [halo_block(): lax.ppermute(ring[-1], 'tile', [(dev, (dev + 1) % 4) for dev in range(4)])]
    unnamed x118 -> x128, local copies, waits for them, and re-layouts: 13.4 us -> 13.9 us
  transfers between devices with their start and end apart: 3 -> 12, of which waited for: 2 -> 8; matrix products, arithmetic and copies ran while one was open for 4% -> 4% of each run, Pallas kernels for 0% -> 0%
where the time goes in v1:
time: 367 us; the launch traced here: 366 us
  waiting for transfers between devices  292 us (80%)
  local copies, waits for them, and re-layouts  29.8 us (8%)
  between operations  19.7 us (5%)
  starting transfers between devices  12.6 us (3%)
  matrix products  6.74 us (2%)
  other arithmetic  5.49 us (1%)
    unnamed x2, waiting for transfers between devices  275 us
    ppermute x9, waiting for transfers between devices, halo_block(): lax.ppermute(ring[-1], 'tile', [(dev, (dev + 1) % 4) for dev in range(4)])  17.1 us
    unnamed x128, local copies, waits for them, and re-layouts  13.9 us
    reshape x1, local copies, waits for them, and re-layouts, every_tap_entries(): block = lax.dot_general(columns, weighting, contract, preferred_element_t...  10.6 us
    ppermute x9, starting transfers between devices, halo_block(): lax.ppermute(ring[-1], 'tile', [(dev, (dev + 1) % 4) for dev in range(4)])  9.99 us
  transfers between devices with their start and end apart: 12, of which 8 were waited for; matrix products, arithmetic and copies ran while one was open for 4% of the time, Pallas kernels for 0%

profile of v1, /device:TPU:0, one launch (start us, length us, event | category | flops | bytes accessed | tf_op | source)
XLA Modules:
  0.0 366.3 jit_solution(10151456996076139771)
XLA Ops:
  8.6 1.0 fusion.18
  9.7 3.0 collective-permute-start
  12.7 1.0 bitcast_select_fusion
  14.4 1.5 collective-permute-start.7
  15.9 1.5 collective-permute-start.1
  17.5 1.7 collective-permute-done.7
  19.7 1.0 collective-permute-done.1
  20.7 1.4 collective-permute-start.2
  22.1 1.4 fusion.34
  26.1 4.4 %copy.47 = bf16[1,27,256,256]{2,3,1,0:T(8,128)(2,1)S(1)} copy(bf16[1,27,256,256]{3,2,1,0:T(8,128)(2,1)} %param.10) | data formatting | bytes 7077888 | tf_op args[2]
  30.5 2.1 rev.3
  32.7 1.4 collective-permute-start.9
  34.1 1.0 maximum_maximum_fusion
  35.1 2.5 collective-permute-done.9
  37.5 1.0 maximum_maximum_fusion.4
  38.6 1.1 maximum_maximum_fusion.5
  40.5 1.4 copy-done
  41.9 0.9 fusion.2
  42.8 1.3 collective-permute-start.3
  45.0 1.2 copy-done.2
  46.2 1.0 fusion.14
  47.8 4.1 %collective-permute-done.4 = bf16[1,3,2,4,256]{4,2,3,1,0:T(2,128)(2,1)S(1)} collective-permute-done((bf16[1,3,2,4,256]{4,2,3,1,0:T(2,128)(2,1)S(1)}, bf16[1,3,2,4,256]{4,2,3,1,0:T(2,128)(2,1)S(1)}, u32[]{:S(2)}, u32[]{:S(2)}) %collective-permute-start.4) | collective-permute-done | bytes 12320 | tf_op jit(solution)/shard_map/ppermute | solution.py:83
  51.9 4.6 %collective-permute-done.5 = bf16[1,3,2,4,256]{4,2,3,1,0:T(2,128)(2,1)S(1)} collective-permute-done((bf16[1,3,2,4,256]{4,2,3,1,0:T(2,128)(2,1)S(1)}, bf16[1,3,2,4,256]{4,2,3,1,0:T(2,128)(2,1)S(1)}, u32[]{:S(2)}, u32[]{:S(2)}) %collective-permute-start.5) | collective-permute-done | bytes 12320 | tf_op jit(solution)/shard_map/ppermute | solution.py:83
  56.5 1.3 collective-permute-start.10
  57.8 3.3 collective-permute-done.6
  62.3 4.0 %convolution_bitcast_fusion = f32[6912,256]{1,0:T(8,128)} fusion(bf16[3,12,4,6912]{3,1,2,0:T(8,128)(2,1)S(1)} %constant_dynamic-update-slice_fusion.54, bf16[3,12,4,256]{3,1,2,0:T(8,128)(2,1)S(1)} %collective-permute-done.10, pred[]{:T(512)S(6)} %eq.5, bf16[1,1,3,12,4,256]{5,4,3,2,1,0:T(4,128)(2,1)S(1)} %copy-done.6, pred[12,4]{0,1:T(4,128)(4,1)S(1)} %broadcast_and_fusion), kind=kOutput, calls=%fused_computation | convolution fusion | flops 509681664 | bytes 9216049 | tf_op jit(solution)/shard_map/dot_general | solution.py:53
  66.3 10.6 %reshape.152 = f32[3,589824]{1,0:T(4,128)} reshape(f32[6912,256]{1,0:T(8,128)} %convolution_bitcast_fusion) | data formatting | bytes 14155776 | tf_op jit(solution)/shard_map/reshape | solution.py:55
  79.5 1.4 copy-done.1
  80.9 0.9 fusion.5
  82.5 274.6 %all-reduce.10.cloned.1.call-done = f32[589824,3]{0,1:T(4,128)} async-done(((f32[589824,3]{0,1:T(4,128)}), f32[589824,3]{0,1:T(4,128)}) %all-reduce.10.cloned.1.call-update) | async-done | bytes 7077904
  357.1 1.2 dynamic-slice_bitcast_fusion
  358.2 1.2 copy.49
  (158 shorter events, 6.9 us)
Async XLA Ops:
  7.2 349.9 %all-reduce.10.cloned.1.call-start = ((), (), s32[]{:S(2)}) async-start(), calls=%async_computation | async-start | bytes 18874368
  9.6 16.4 %copy-start.3 = (bf16[3,12,4,256]{3,1,2,0:T(8,128)(2,1)}, bf16[3,12,4,256]{3,1,2,0:T(8,128)(2,1)S(1)}, u32[]{:S(2)}) copy-start(bf16[3,12,4,256]{3,1,2,0:T(8,128)(2,1)S(1)} %fusion.18) | copy-start | bytes 221188
  9.7 6.2 %collective-permute-start = (bf16[1,3,2,4,256]{4,2,3,1,0:T(2,128)(2,1)S(1)}, bf16[1,3,2,4,256]{4,2,3,1,0:T(2,128)(2,1)S(1)}, u32[]{:S(2)}, u32[]{:S(2)}) collective-permute-start(bf16[1,3,2,4,256]{4,2,3,1,0:T(2,128)(2,1)S(1)} %maximum_bitcast_fusion), channel_id=1, source_target_pairs={{0,1},{1,2},{2,3},{3,0},{4,5},{5,6},{6,7},{7,4},{8,9},{9,10},{10,1... | collective-permute-start | bytes 36872 | tf_op jit(solution)/shard_map/ppermute | solution.py:83
  13.7 0.6 copy-start.4
  14.4 1.6 copy-start.7
  14.4 4.8 %collective-permute-start.7 = (bf16[1,3,2,4,256]{4,2,3,1,0:T(2,128)(2,1)S(1)}, bf16[1,3,2,4,256]{4,2,3,1,0:T(2,128)(2,1)}, u32[]{:S(2)}, u32[]{:S(2)}) collective-permute-start(bf16[1,3,2,4,256]{4,2,3,1,0:T(2,128)(2,1)S(1)} %maximum_bitcast_fusion.2), channel_id=1, source_target_pairs={{0,1},{1,2},{2,3},{3,0},{4,5},{5,6},{6,7},{7,4},{8,9},{9,10},{10,1... | collective-permute-start | bytes 36872 | tf_op jit(solution)/shard_map/ppermute | solution.py:83
  15.9 3.2 copy-start.8
  15.9 4.7 %collective-permute-start.1 = (bf16[1,3,2,4,256]{4,2,3,1,0:T(2,128)(2,1)S(1)}, bf16[1,3,2,4,256]{4,2,3,1,0:T(2,128)(2,1)}, u32[]{:S(2)}, u32[]{:S(2)}) collective-permute-start(bf16[1,3,2,4,256]{4,2,3,1,0:T(2,128)(2,1)S(1)} %collective-permute-done), channel_id=1, source_target_pairs={{0,1},{1,2},{2,3},{3,0},{4,5},{5,6},{6,7},{7,4},{8,9},{9,10},{10,1... | collective-permute-start | bytes 36872 | tf_op jit(solution)/shard_map/ppermute | solution.py:83
  19.1 13.6 %collective-permute-start.8 = (bf16[1,3,2,4,256]{4,2,3,1,0:T(2,128)(2,1)}, bf16[1,3,2,4,256]{4,2,3,1,0:T(2,128)(2,1)}, u32[]{:S(2)}, u32[]{:S(2)}) collective-permute-start(bf16[1,3,2,4,256]{4,2,3,1,0:T(2,128)(2,1)} %collective-permute-done.7), channel_id=1, source_target_pairs={{0,1},{1,2},{2,3},{3,0},{4,5},{5,6},{6,7},{7,4},{8,9},{9,10},{10,1... | collective-permute-start | bytes 36872 | tf_op jit(solution)/shard_map/ppermute | solution.py:83
  20.7 13.4 %collective-permute-start.2 = (bf16[1,3,2,4,256]{4,2,3,1,0:T(2,128)(2,1)}, bf16[1,3,2,4,256]{4,2,3,1,0:T(2,128)(2,1)}, u32[]{:S(2)}, u32[]{:S(2)}) collective-permute-start(bf16[1,3,2,4,256]{4,2,3,1,0:T(2,128)(2,1)} %collective-permute-done.1), channel_id=1, source_target_pairs={{0,1},{1,2},{2,3},{3,0},{4,5},{5,6},{6,7},{7,4},{8,9},{9,10},{10,1... | collective-permute-start | bytes 36872 | tf_op jit(solution)/shard_map/ppermute | solution.py:83
  32.7 4.8 %collective-permute-start.9 = (bf16[1,3,2,4,256]{4,2,3,1,0:T(2,128)(2,1)}, bf16[1,3,2,4,256]{4,2,3,1,0:T(2,128)(2,1)S(1)}, u32[]{:S(2)}, u32[]{:S(2)}) collective-permute-start(bf16[1,3,2,4,256]{4,2,3,1,0:T(2,128)(2,1)} %collective-permute-done.8), channel_id=1, source_target_pairs={{0,1},{1,2},{2,3},{3,0},{4,5},{5,6},{6,7},{7,4},{8,9},{9,10},{10,1... | collective-permute-start | bytes 36872 | tf_op jit(solution)/shard_map/ppermute | solution.py:83
  39.9 2.0 copy-start
  39.9 2.0 copy-start.5
  42.8 2.2 collective-permute-start.3
  44.2 2.0 copy-start.2
  44.2 2.0 copy-start.6
  47.2 4.6 %collective-permute-start.4 = (bf16[1,3,2,4,256]{4,2,3,1,0:T(2,128)(2,1)S(1)}, bf16[1,3,2,4,256]{4,2,3,1,0:T(2,128)(2,1)S(1)}, u32[]{:S(2)}, u32[]{:S(2)}) collective-permute-start(bf16[1,3,2,4,256]{4,2,3,1,0:T(2,128)(2,1)S(1)} %maximum_bitcast_fusion.1), channel_id=1, source_target_pairs={{0,1},{1,2},{2,3},{3,0},{4,5},{5,6},{6,7},{7,4},{8,9},{9,10},{10,1... | collective-permute-start | bytes 36872 | tf_op jit(solution)/shard_map/ppermute | solution.py:83
  51.9 4.6 %collective-permute-start.5 = (bf16[1,3,2,4,256]{4,2,3,1,0:T(2,128)(2,1)S(1)}, bf16[1,3,2,4,256]{4,2,3,1,0:T(2,128)(2,1)S(1)}, u32[]{:S(2)}, u32[]{:S(2)}) collective-permute-start(bf16[1,3,2,4,256]{4,2,3,1,0:T(2,128)(2,1)S(1)} %collective-permute-done.4), channel_id=1, source_target_pairs={{0,1},{1,2},{2,3},{3,0},{4,5},{5,6},{6,7},{7,4},{8,9},{9,10},{10,1... | collective-permute-start | bytes 36872 | tf_op jit(solution)/shard_map/ppermute | solution.py:83
  56.5 4.6 %collective-permute-start.6 = (bf16[1,3,2,4,256]{4,2,3,1,0:T(2,128)(2,1)S(1)}, bf16[1,3,2,4,256]{4,2,3,1,0:T(2,128)(2,1)S(1)}, u32[]{:S(2)}, u32[]{:S(2)}) collective-permute-start(bf16[1,3,2,4,256]{4,2,3,1,0:T(2,128)(2,1)S(1)} %collective-permute-done.5), channel_id=1, source_target_pairs={{0,1},{1,2},{2,3},{3,0},{4,5},{5,6},{6,7},{7,4},{8,9},{9,10},{10,1... | collective-permute-start | bytes 36872 | tf_op jit(solution)/shard_map/ppermute | solution.py:83
  56.5 5.8 %collective-permute-start.10 = (bf16[3,12,4,256]{3,1,2,0:T(8,128)(2,1)S(1)}, bf16[3,12,4,256]{3,1,2,0:T(8,128)(2,1)S(1)}, u32[]{:S(2)}, u32[]{:S(2)}) collective-permute-start(bf16[3,12,4,256]{3,1,2,0:T(8,128)(2,1)S(1)} %get-tuple-element.11), channel_id=1, source_target_pairs={{16,0},{17,1},{18,2},{19,3},{20,4},{21,5},{22,6},{23,7},{24,8},{25... | collective-permute-start | bytes 221192 | tf_op jit(solution)/shard_map/ppermute | solution.py:10
  77.0 0.7 copy-start.9
  78.9 2.0 copy-start.1
Sparse Core Ops, SparseCore 0:
  77.1 279.9 all-reduce.9
